TPU v7x, 32 devices: a whole 2x2x4 slice. The times are simulated.
32 devices in a mesh: dp: 2 (over y), section: 4 (over z), mp: 4 (over x, core).
Axes of the slice: x: 2, y: 2, z: 4, core: 2. Of those that a mesh axis runs over, the one named last changes fastest.
Arguments:
- token_ids: int32 [32, 32], P('dp'), may hold values from 0 to 65535
- members: int32 [32], replicated, may hold values from 0 to 31, each once
- owners: int32 [4], replicated, may hold values from 0 to 3, each once
- embed_table: bfloat16 [4096, 65536], P('mp', 'section'), may hold values from -6 to 6
- norm_gain: float32 [4, 4096], P('section'), may hold values from 0.5 to 2
- gate_weight: bfloat16 [4, 4096, 10240], P('section', None, 'mp'), may hold values from -0.09375 to 0.09375
- up_weight: bfloat16 [4, 4096, 10240], P('section', None, 'mp'), may hold values from -0.09375 to 0.09375
- down_weight: bfloat16 [4, 4096, 10240], P('section', None, 'mp'), may hold values from -0.078125 to 0.078125
- final_gain: float32 [4096], replicated, may hold values from 0.5 to 2
- head_weight: bfloat16 [4096, 4096], P(None, 'mp'), may hold values from -0.0014648438 to 0.0014648438
Outputs:
- wins: float32 [4, 8, 8], P('dp', 'section')
Inputs may be any that keep to these rules, and one draw needn't show every extreme that they name: Prompt p's responses are members[8 * p] to members[8 * p + 7]; each response belongs to one prompt. `owners`: each slot holds one prompt.
All inputs are finite; a program needn't handle non-finite values.
Results may differ from a plain program's by a relative error of at most 0.028.
Values may be sent and summed in bfloat16 or wider, within the bound.
A program may use at most 192 MiB of HBM per device.

v0:
```python
import jax
import jax.numpy as jnp
from jax import lax
from jax.sharding import PartitionSpec as P

GROUP = 8


norm_eps = 1e-05
final_eps = 1e-06


def passed_along(value, axis, steps):
    count = lax.axis_size(axis)
    leading, last = (max(0, -steps), min(count, count - steps))
    return lax.ppermute(value, axis, [(source, source + steps) for source in range(leading, last)])


def broadcast(block, axis, source):
    block = jnp.where(lax.axis_index(axis) == source, block, jnp.zeros_like(block))
    return lax.psum(block, axis)


def contract_rows(weights, acts):
    return lax.dot_general(
        weights, acts, (((0,), (0,)), ((), ())), preferred_element_type=jnp.float32
    )


def activate(gate_acc, up_acc, squares, width):
    inverse = lax.rsqrt(squares / width + norm_eps)
    return (jax.nn.silu(gate_acc * inverse) * (up_acc * inverse)).astype(jnp.bfloat16)


def layer_split(state, gain, w_gate, w_up, w_down):
    width = gain.shape[0]
    wide = lax.all_gather(state, "mp", axis=0, tiled=True).astype(jnp.float32)
    scaled = (wide * gain[:, None]).astype(jnp.bfloat16)
    gate_acc = contract_rows(w_gate, scaled)
    up_acc = contract_rows(w_up, scaled)
    squares = jnp.sum(wide * wide, axis=0, keepdims=True)
    gate_acc, up_acc, squares = (gate_acc, up_acc, squares)
    hidden = activate(gate_acc, up_acc, squares, width)
    mixed = lax.psum_scatter(
        jnp.dot(w_down, hidden, preferred_element_type=jnp.float32).astype(jnp.bfloat16),
        "mp",
        scatter_dimension=0,
        tiled=True,
    ).astype(jnp.float32)
    return (state.astype(jnp.float32) + mixed).astype(jnp.bfloat16)


def per_device(
    token_ids,
    members,
    owners,
    embed_table,
    norm_gain,
    gate_weight,
    up_weight,
    down_weight,
    final_gain,
    head_weight,
):
    sections = lax.axis_size("section")
    section = lax.axis_index("section")
    vocab_part = embed_table.shape[1]
    flat = token_ids.reshape(-1)
    local_ids = flat - section * vocab_part
    inside = (local_ids >= 0) & (local_ids < vocab_part)
    picked = jnp.take(embed_table, jnp.clip(local_ids, 0, vocab_part - 1), axis=1)
    partial_value = jnp.where(inside[None, :], picked.astype(jnp.float32), 0.0)
    embedded = lax.psum(partial_value.astype(jnp.bfloat16), "section")
    gain = norm_gain[0]
    w_gate = gate_weight[0]
    w_up = up_weight[0]
    w_down = down_weight[0]
    block = embedded.shape[1] // sections
    state = jnp.zeros((embedded.shape[0], block), jnp.bfloat16)
    finished = []
    for tick in range(sections + sections - 1):
        if tick < sections:
            fresh = embedded[:, tick * block : (tick + 1) * block]
            state = jnp.where(section == 0, fresh, state)
        result = layer_split(state, gain, w_gate, w_up, w_down)
        if tick >= sections - 1:
            finished.append(result)
        if tick < sections + sections - 2:
            state = passed_along(result, "section", 1)
    final = jnp.concatenate(finished, axis=1)
    responses_here = token_ids.shape[0]
    length = token_ids.shape[1]
    pooled = jnp.mean(
        final.astype(jnp.float32).reshape(final.shape[0], responses_here, length), axis=2
    )
    groups_count = lax.axis_size("dp")
    parts = lax.axis_size("mp")
    stacked = lax.all_gather(pooled[None], ("dp", "mp"), axis=0, tiled=True)
    stacked = stacked.reshape(groups_count, parts, pooled.shape[0], responses_here)
    everyone = jnp.transpose(stacked, (1, 2, 0, 3)).reshape(
        parts * pooled.shape[0], groups_count * responses_here
    )
    factor = lax.rsqrt(jnp.mean(everyone * everyone, axis=0, keepdims=True) + final_eps)
    normed = (everyone * factor * final_gain[:, None]).astype(jnp.bfloat16)
    head_cols = head_weight.shape[1]
    projected = contract_rows(head_weight, normed)
    mine = lax.dynamic_slice_in_dim(normed, lax.axis_index("mp") * head_cols, head_cols).astype(
        jnp.float32
    )
    partial_scores = lax.dot_general(
        projected,
        mine,
        (((0,), (0,)), ((), ())),
        precision=lax.Precision.HIGHEST,
        preferred_element_type=jnp.float32,
    )
    scores = lax.psum(partial_scores, "mp")
    scores = broadcast(scores, "section", sections - 1)
    preference = jax.nn.sigmoid(scores - scores.T)
    prompt_count = owners.shape[0]
    local_prompts = prompt_count // lax.axis_size("dp")
    rows_local = GROUP // sections
    slot_here = lax.axis_index("dp") * local_prompts + jnp.arange(local_prompts, dtype=jnp.int32)
    match = (owners[None, :] == slot_here[:, None]).astype(jnp.int32)
    prompt_here = jnp.sum(match * jnp.arange(prompt_count, dtype=jnp.int32)[None, :], axis=1)
    groups = members.reshape(prompt_count, GROUP)
    chosen = groups[prompt_here]
    row_ids = lax.dynamic_slice_in_dim(chosen, section * rows_local, rows_local, 1)
    return preference[row_ids[:, :, None], chosen[:, None, :]]


def solution(mesh):
    placed = (
        P("dp", None),
        P(),
        P(),
        P("mp", "section"),
        P("section", None),
        P("section", None, "mp"),
        P("section", None, "mp"),
        P("section", None, "mp"),
        P(),
        P(None, "mp"),
    )
    return jax.shard_map(
        per_device, mesh=mesh, in_specs=placed, out_specs=P("dp", "section", None), check_vma=False
    )
```

profile of v0, /device:TPU:0, one launch (start us, length us, event | category | flops | bytes accessed | tf_op | source)
XLA Modules:
  0.0 752.6 jit_solution(12075295378497106360)
XLA Ops:
  8.2 43.9 %copy.26 = bf16[1024,16384]{0,1:T(8,128)(2,1)} copy(bf16[1024,16384]{1,0:T(8,128)(2,1)} %param.13) | data formatting | bytes 67108864 | tf_op args[3]
  52.1 16.2 %gather_fusion = bf16[512,1024]{1,0:T(8,128)(2,1)S(1)} fusion(bf16[1024,16384]{0,1:T(8,128)(2,1)} %copy.26, s32[1024]{0:T(1024)S(1)} %pad_clamp_fusion.1), kind=kCustom, calls=%fused_computation | custom fusion | bytes 2099200 | tf_op jit(solution)/shard_map/jit(_take)/gather | solution.py:71
  68.4 1.3 fusion.273
  69.7 55.0 %all-reduce.2.cloned.1.call-done = bf16[1024,512]{0,1:T(8,128)(2,1)} async-done(((bf16[1024,512]{0,1:T(8,128)(2,1)}), bf16[1024,512]{0,1:T(8,128)(2,1)}) %all-reduce.2.cloned.1.call-update) | async-done | bytes 1048592 | tf_op jit(solution)/shard_map/psum | solution.py:73
  124.7 1.7 slice_select_fusion
  126.5 16.1 %all-gather.9.cloned.1.call-done = bf16[4096,128]{0,1:T(8,128)(2,1)} async-done(((bf16[1024,128]{0,1:T(8,128)(2,1)}), bf16[4096,128]{0,1:T(8,128)(2,1)}) %all-gather.9.cloned.1.call-update) | async-done | bytes 1048592 | tf_op jit(solution)/shard_map/all_gather | solution.py:37
  142.5 1.5 fusion.211
  144.1 11.3 %fusion.87 = f32[2560,128]{0,1:T(8,128)} fusion(bf16[1,4096,2560]{2,1,0:T(8,128)(2,1)} %param.15, bf16[4096,128]{0,1:T(8,128)(2,1)} %all-gather.9.cloned.1.call-done, f32[4096]{0:T(1024)S(1)} %bitcast.292, f32[128]{0:T(128)S(1)} %add_rsqrt_fusion.7), kind=kOutput, calls=%fused_computation.60 | convolution fusion | flops 2686255104 | bytes 23347712 | tf_op jit(solution)/shard_map/dot_general | solution.py:25
  155.4 18.6 %fusion.81 = bf16[4096,128]{0,1:T(8,128)(2,1)} fusion(bf16[1,4096,2560]{2,1,0:T(8,128)(2,1)} %param.17, bf16[1,4096,2560]{2,1,0:T(8,128)(2,1)} %param.16, f32[2560,128]{0,1:T(8,128)} %fusion.87, bf16[4096,128]{0,1:T(8,128)(2,1)S(1)} %copy-done, f32[4096]{0:T(1024)S(1)} %bitcast.293, f32[128]{0:T(128)S(1)} %add_rsqrt_fusion.7), kind=kOutput, calls=%fused_computation.58 | convolution fusion | flops 5373100032 | bytes 45367808 | tf_op jit(solution)/shard_map/dot_general | solution.py:45
  174.1 24.9 %reduce-scatter.8.cloned.1.call-done = bf16[1024,128]{0,1:T(8,128)(2,1)} async-done(((bf16[4096,128]{0,1:T(8,128)(2,1)}), bf16[1024,128]{0,1:T(8,128)(2,1)}) %reduce-scatter.8.cloned.1.call-update) | async-done | bytes 262160 | tf_op jit(solution)/shard_map/reduce_scatter | solution.py:44
  198.9 1.0 add_convert_fusion.6
  200.0 3.4 collective-permute-start
  203.4 5.4 collective-permute-done
  209.8 17.6 %all-gather.11.cloned.1.call-done = bf16[4096,128]{0,1:T(8,128)(2,1)} async-done(((bf16[1024,128]{0,1:T(8,128)(2,1)}), bf16[4096,128]{0,1:T(8,128)(2,1)}) %all-gather.11.cloned.1.call-update) | async-done | bytes 1048592 | tf_op jit(solution)/shard_map/all_gather | solution.py:37
  227.4 1.5 fusion.213
  228.9 11.3 %fusion.93 = f32[2560,128]{0,1:T(8,128)} fusion(bf16[1,4096,2560]{2,1,0:T(8,128)(2,1)} %param.15, bf16[4096,128]{0,1:T(8,128)(2,1)} %all-gather.11.cloned.1.call-done, f32[4096]{0:T(1024)S(1)} %bitcast.294, f32[128]{0:T(128)S(1)} %add_rsqrt_fusion.6), kind=kOutput, calls=%fused_computation.62 | convolution fusion | flops 2686255104 | bytes 23347712 | tf_op jit(solution)/shard_map/dot_general | solution.py:25
  240.3 18.5 %fusion.78 = bf16[4096,128]{0,1:T(8,128)(2,1)} fusion(bf16[1,4096,2560]{2,1,0:T(8,128)(2,1)} %param.17, bf16[1,4096,2560]{2,1,0:T(8,128)(2,1)} %param.16, f32[2560,128]{0,1:T(8,128)} %fusion.93, bf16[4096,128]{0,1:T(8,128)(2,1)S(1)} %copy-done.1, f32[4096]{0:T(1024)S(1)} %bitcast.295, f32[128]{0:T(128)S(1)} %add_rsqrt_fusion.6), kind=kOutput, calls=%fused_computation.57 | convolution fusion | flops 5373100032 | bytes 45367808 | tf_op jit(solution)/shard_map/dot_general | solution.py:45
  258.8 24.9 %reduce-scatter.10.cloned.1.call-done = bf16[1024,128]{0,1:T(8,128)(2,1)} async-done(((bf16[4096,128]{0,1:T(8,128)(2,1)}), bf16[1024,128]{0,1:T(8,128)(2,1)}) %reduce-scatter.10.cloned.1.call-update) | async-done | bytes 262160 | tf_op jit(solution)/shard_map/reduce_scatter | solution.py:44
  283.8 1.0 add_convert_fusion.5
  284.8 3.4 collective-permute-start.1
  288.2 5.4 collective-permute-done.1
  294.4 17.8 %all-gather.13.cloned.1.call-done = bf16[4096,128]{0,1:T(8,128)(2,1)} async-done(((bf16[1024,128]{0,1:T(8,128)(2,1)}), bf16[4096,128]{0,1:T(8,128)(2,1)}) %all-gather.13.cloned.1.call-update) | async-done | bytes 1048592 | tf_op jit(solution)/shard_map/all_gather | solution.py:37
  312.2 1.5 fusion.215
  313.7 11.3 %fusion.99 = f32[2560,128]{0,1:T(8,128)} fusion(bf16[1,4096,2560]{2,1,0:T(8,128)(2,1)} %param.15, bf16[4096,128]{0,1:T(8,128)(2,1)} %all-gather.13.cloned.1.call-done, f32[4096]{0:T(1024)S(1)} %bitcast.296, f32[128]{0:T(128)S(1)} %add_rsqrt_fusion.5), kind=kOutput, calls=%fused_computation.64 | convolution fusion | flops 2686255104 | bytes 23347712 | tf_op jit(solution)/shard_map/dot_general | solution.py:25
  325.0 18.5 %fusion.75 = bf16[4096,128]{0,1:T(8,128)(2,1)} fusion(bf16[1,4096,2560]{2,1,0:T(8,128)(2,1)} %param.17, bf16[1,4096,2560]{2,1,0:T(8,128)(2,1)} %param.16, f32[2560,128]{0,1:T(8,128)} %fusion.99, bf16[4096,128]{0,1:T(8,128)(2,1)S(1)} %copy-done.2, f32[4096]{0:T(1024)S(1)} %bitcast.297, f32[128]{0:T(128)S(1)} %add_rsqrt_fusion.5), kind=kOutput, calls=%fused_computation.56 | convolution fusion | flops 5373100032 | bytes 45367808 | tf_op jit(solution)/shard_map/dot_general | solution.py:45
  343.8 24.7 %reduce-scatter.12.cloned.1.call-done = bf16[1024,128]{0,1:T(8,128)(2,1)} async-done(((bf16[4096,128]{0,1:T(8,128)(2,1)}), bf16[1024,128]{0,1:T(8,128)(2,1)}) %reduce-scatter.12.cloned.1.call-update) | async-done | bytes 262160 | tf_op jit(solution)/shard_map/reduce_scatter | solution.py:44
  368.5 1.0 add_convert_fusion.4
  369.5 3.4 collective-permute-start.2
  373.0 5.3 collective-permute-done.2
  378.3 0.7 slice_select_fusion.3
  379.1 17.8 %all-gather.15.cloned.1.call-done = bf16[4096,128]{0,1:T(8,128)(2,1)} async-done(((bf16[1024,128]{0,1:T(8,128)(2,1)}), bf16[4096,128]{0,1:T(8,128)(2,1)}) %all-gather.15.cloned.1.call-update) | async-done | bytes 1048592 | tf_op jit(solution)/shard_map/all_gather | solution.py:37
  397.0 1.5 fusion.217
  398.5 8.9 %fusion.105 = f32[2560,128]{0,1:T(8,128)S(1)} fusion(bf16[1,4096,2560]{2,1,0:T(8,128)(2,1)} %param.15, bf16[4096,128]{0,1:T(8,128)(2,1)} %all-gather.15.cloned.1.call-done, f32[4096]{0:T(1024)S(1)} %bitcast.298, f32[128]{0:T(128)S(1)} %add_rsqrt_fusion.4), kind=kOutput, calls=%fused_computation.66 | convolution fusion | flops 2686255104 | bytes 23347712 | tf_op jit(solution)/shard_map/dot_general | solution.py:25
  407.4 18.3 %fusion.72 = bf16[4096,128]{0,1:T(8,128)(2,1)} fusion(bf16[1,4096,2560]{2,1,0:T(8,128)(2,1)} %param.17, bf16[1,4096,2560]{2,1,0:T(8,128)(2,1)} %param.16, f32[2560,128]{0,1:T(8,128)S(1)} %fusion.105, bf16[4096,128]{0,1:T(8,128)(2,1)S(1)} %copy-done.3, f32[4096]{0:T(1024)S(1)} %bitcast.299, f32[128]{0:T(128)S(1)} %add_rsqrt_fusion.4), kind=kOutput, calls=%fused_computation.55 | convolution fusion | flops 5373100032 | bytes 45367808 | tf_op jit(solution)/shard_map/dot_general | solution.py:45
  425.8 24.9 %reduce-scatter.14.cloned.1.call-done = bf16[1024,128]{0,1:T(8,128)(2,1)} async-done(((bf16[4096,128]{0,1:T(8,128)(2,1)}), bf16[1024,128]{0,1:T(8,128)(2,1)}) %reduce-scatter.14.cloned.1.call-update) | async-done | bytes 262160 | tf_op jit(solution)/shard_map/reduce_scatter | solution.py:44
  450.7 1.0 add_convert_fusion.3
  451.7 3.4 collective-permute-start.3
  455.1 5.4 collective-permute-done.3
  461.3 17.8 %all-gather.17.cloned.1.call-done = bf16[4096,128]{0,1:T(8,128)(2,1)} async-done(((bf16[1024,128]{0,1:T(8,128)(2,1)}), bf16[4096,128]{0,1:T(8,128)(2,1)}) %all-gather.17.cloned.1.call-update) | async-done | bytes 1048592 | tf_op jit(solution)/shard_map/all_gather | solution.py:37
  479.1 1.5 fusion.219
  480.6 8.9 %fusion.111 = f32[2560,128]{0,1:T(8,128)S(1)} fusion(bf16[1,4096,2560]{2,1,0:T(8,128)(2,1)} %param.15, bf16[4096,128]{0,1:T(8,128)(2,1)} %all-gather.17.cloned.1.call-done, f32[4096]{0:T(1024)S(1)} %bitcast.300, f32[128]{0:T(128)S(1)} %add_rsqrt_fusion.3), kind=kOutput, calls=%fused_computation.68 | convolution fusion | flops 2686255104 | bytes 23347712 | tf_op jit(solution)/shard_map/dot_general | solution.py:25
  489.5 18.3 %fusion.69 = bf16[4096,128]{0,1:T(8,128)(2,1)} fusion(bf16[1,4096,2560]{2,1,0:T(8,128)(2,1)} %param.17, bf16[1,4096,2560]{2,1,0:T(8,128)(2,1)} %param.16, f32[2560,128]{0,1:T(8,128)S(1)} %fusion.111, bf16[4096,128]{0,1:T(8,128)(2,1)S(1)} %copy-done.4, f32[4096]{0:T(1024)S(1)} %bitcast.301, f32[128]{0:T(128)S(1)} %add_rsqrt_fusion.3), kind=kOutput, calls=%fused_computation.54 | convolution fusion | flops 5373100032 | bytes 45367808 | tf_op jit(solution)/shard_map/dot_general | solution.py:45
  507.9 24.9 %reduce-scatter.16.cloned.1.call-done = bf16[1024,128]{0,1:T(8,128)(2,1)} async-done(((bf16[4096,128]{0,1:T(8,128)(2,1)}), bf16[1024,128]{0,1:T(8,128)(2,1)}) %reduce-scatter.16.cloned.1.call-update) | async-done | bytes 262160 | tf_op jit(solution)/shard_map/reduce_scatter | solution.py:44
  532.8 1.0 add_convert_fusion.2
  533.8 3.4 collective-permute-start.4
  537.3 5.4 collective-permute-done.4
  543.7 17.6 %all-gather.19.cloned.1.call-done = bf16[4096,128]{0,1:T(8,128)(2,1)} async-done(((bf16[1024,128]{0,1:T(8,128)(2,1)}), bf16[4096,128]{0,1:T(8,128)(2,1)}) %all-gather.19.cloned.1.call-update) | async-done | bytes 1048592 | tf_op jit(solution)/shard_map/all_gather | solution.py:37
  561.2 1.5 fusion.221
  562.8 8.9 %fusion.117 = f32[2560,128]{0,1:T(8,128)S(1)} fusion(bf16[1,4096,2560]{2,1,0:T(8,128)(2,1)} %param.15, bf16[4096,128]{0,1:T(8,128)(2,1)} %all-gather.19.cloned.1.call-done, f32[4096]{0:T(1024)S(1)} %bitcast.302, f32[128]{0:T(128)S(1)} %add_rsqrt_fusion.2), kind=kOutput, calls=%fused_computation.70 | convolution fusion | flops 2686255104 | bytes 23347712 | tf_op jit(solution)/shard_map/dot_general | solution.py:25
  571.7 18.3 %fusion.66 = bf16[4096,128]{0,1:T(8,128)(2,1)} fusion(bf16[1,4096,2560]{2,1,0:T(8,128)(2,1)} %param.17, bf16[1,4096,2560]{2,1,0:T(8,128)(2,1)} %param.16, f32[2560,128]{0,1:T(8,128)S(1)} %fusion.117, bf16[4096,128]{0,1:T(8,128)(2,1)S(1)} %copy-done.5, f32[4096]{0:T(1024)S(1)} %bitcast.303, f32[128]{0:T(128)S(1)} %add_rsqrt_fusion.2), kind=kOutput, calls=%fused_computation.53 | convolution fusion | flops 5373100032 | bytes 45367808 | tf_op jit(solution)/shard_map/dot_general | solution.py:45
  590.1 24.9 %reduce-scatter.18.cloned.1.call-done = bf16[1024,128]{0,1:T(8,128)(2,1)} async-done(((bf16[4096,128]{0,1:T(8,128)(2,1)}), bf16[1024,128]{0,1:T(8,128)(2,1)}) %reduce-scatter.18.cloned.1.call-update) | async-done | bytes 262160 | tf_op jit(solution)/shard_map/reduce_scatter | solution.py:44
  615.0 1.0 add_convert_fusion.1
  616.0 3.4 collective-permute-start.5
  619.4 5.4 collective-permute-done.5
  625.5 17.8 %all-gather.21.cloned.1.call-done = bf16[4096,128]{0,1:T(8,128)(2,1)} async-done(((bf16[1024,128]{0,1:T(8,128)(2,1)}), bf16[4096,128]{0,1:T(8,128)(2,1)}) %all-gather.21.cloned.1.call-update) | async-done | bytes 1048592 | tf_op jit(solution)/shard_map/all_gather | solution.py:37
  643.4 1.5 fusion.223
  644.9 8.9 %fusion.123 = f32[2560,128]{0,1:T(8,128)S(1)} fusion(bf16[1,4096,2560]{2,1,0:T(8,128)(2,1)} %param.15, bf16[4096,128]{0,1:T(8,128)(2,1)} %all-gather.21.cloned.1.call-done, f32[4096]{0:T(1024)S(1)} %bitcast.304, f32[128]{0:T(128)S(1)} %add_rsqrt_fusion.1), kind=kOutput, calls=%fused_computation.72 | convolution fusion | flops 2686255104 | bytes 23347712 | tf_op jit(solution)/shard_map/dot_general | solution.py:25
  653.9 18.3 %fusion.63 = bf16[4096,128]{0,1:T(8,128)(2,1)} fusion(bf16[1,4096,2560]{2,1,0:T(8,128)(2,1)} %param.17, bf16[1,4096,2560]{2,1,0:T(8,128)(2,1)} %param.16, f32[2560,128]{0,1:T(8,128)S(1)} %fusion.123, bf16[4096,128]{0,1:T(8,128)(2,1)S(1)} %copy-done.6, f32[4096]{0:T(1024)S(1)} %bitcast.305, f32[128]{0:T(128)S(1)} %add_rsqrt_fusion.1), kind=kOutput, calls=%fused_computation.52 | convolution fusion | flops 5373100032 | bytes 45367808 | tf_op jit(solution)/shard_map/dot_general | solution.py:45
  673.3 23.8 %reduce-scatter.20.cloned.1.call-done = bf16[1024,128]{0,1:T(8,128)(2,1)} async-done(((bf16[4096,128]{0,1:T(8,128)(2,1)}), bf16[1024,128]{0,1:T(8,128)(2,1)}) %reduce-scatter.20.cloned.1.call-update) | async-done | bytes 262160 | tf_op jit(solution)/shard_map/reduce_scatter | solution.py:44
  697.1 1.0 add_convert_fusion
  698.4 10.1 %all-gather = f32[8192,16]{0,1:T(8,128)S(1)} all-gather(f32[1024,16]{0,1:T(8,128)S(1)} %broadcast_multiply_fusion), channel_id=2, replica_groups=mesh['dp'=2,'section'=4,'mp'=4] {'dp','mp'}, dimensions={0}, use_global_device_ids=true | all-gather | bytes 589824 | tf_op jit(solution)/shard_map/all_gather | solution.py:98
  709.8 4.9 fusion.329
  714.9 10.5 %psum.22 = f32[32,32]{1,0:T(8,128)S(1)} all-reduce(f32[32,32]{1,0:T(8,128)S(1)} %fusion.309), channel_id=1, replica_groups=mesh['dp'=2,'section'=4,'mp'=4] {'mp'}, use_global_device_ids=true, to_apply=%region_17.18 | all-reduce | flops 1024 | bytes 8192 | tf_op jit(solution)/shard_map/psum | solution.py:117
  725.4 18.7 %psum.23 = f32[32,32]{1,0:T(8,128)S(1)} all-reduce(f32[32,32]{1,0:T(8,128)S(1)} %broadcast_select_fusion), channel_id=1, replica_groups=mesh['dp'=2,'section'=4,'mp'=4] {'section'}, use_global_device_ids=true, to_apply=%region_18.19 | all-reduce | flops 1024 | bytes 8192 | tf_op jit(solution)/shard_map/psum | solution.py:21
  (115 shorter events, 11.1 us)
Async XLA Ops:
  6.5 118.2 %all-reduce.2.cloned.1.call-start = ((), (), s32[]{:S(2)}) async-start(), calls=%async_computation.7 | async-start | bytes 2097152 | tf_op jit(solution)/shard_map/psum | solution.py:73
  68.4 75.7 %copy-start.7 = (f32[1,4096]{1,0:T(1,128)S(1)}, f32[1,4096]{1,0:T(1,128)}, u32[]{:S(2)}) copy-start(f32[1,4096]{1,0:T(1,128)} %param.14) | copy-start | bytes 49156
  69.7 72.8 %all-gather.9.cloned.1.call-start = ((), (), s32[]{:S(2)}) async-start(), calls=%async_computation.8 | async-start | bytes 1310720 | tf_op jit(solution)/shard_map/all_gather | solution.py:37
  126.4 72.5 %reduce-scatter.8.cloned.1.call-start = ((), (), s32[]{:S(2)}) async-start(), calls=%async_computation.9 | async-start | bytes 1310720 | tf_op jit(solution)/shard_map/reduce_scatter | solution.py:44
  144.1 11.4 %copy-start = (bf16[4096,128]{0,1:T(8,128)(2,1)S(1)}, bf16[4096,128]{0,1:T(8,128)(2,1)}, u32[]{:S(2)}) copy-start(bf16[4096,128]{0,1:T(8,128)(2,1)} %all-gather.9.cloned.1.call-done) | copy-start | bytes 3145732
  155.4 43.5 %copy-start.11 = (bf16[1024,512]{0,1:T(8,128)(2,1)S(1)}, bf16[1024,512]{0,1:T(8,128)(2,1)}, u32[]{:S(2)}) copy-start(bf16[1024,512]{0,1:T(8,128)(2,1)} %all-reduce.2.cloned.1.call-done) | copy-start | bytes 3145732
  174.0 53.4 %all-gather.11.cloned.1.call-start = ((), (), s32[]{:S(2)}) async-start(), calls=%async_computation.10 | async-start | bytes 1310720 | tf_op jit(solution)/shard_map/all_gather | solution.py:37
  200.0 8.8 %collective-permute-start = (bf16[1024,128]{0,1:T(8,128)(2,1)S(1)}, bf16[1024,128]{0,1:T(8,128)(2,1)S(1)}, u32[]{:S(2)}, u32[]{:S(2)}) collective-permute-start(bf16[1024,128]{0,1:T(8,128)(2,1)S(1)} %add_convert_fusion.6), channel_id=1, source_target_pairs={{0,4},{4,8},{8,12},{1,5},{5,9},{9,13},{2,6},{6,10},{10,14},{3,7},{... | collective-permute-start | bytes 786440 | tf_op jit(solution)/shard_map/ppermute | solution.py:16
  209.5 74.2 %reduce-scatter.10.cloned.1.call-start = ((), (), s32[]{:S(2)}) async-start(), calls=%async_computation.11 | async-start | bytes 1310720 | tf_op jit(solution)/shard_map/reduce_scatter | solution.py:44
  228.9 11.4 %copy-start.1 = (bf16[4096,128]{0,1:T(8,128)(2,1)S(1)}, bf16[4096,128]{0,1:T(8,128)(2,1)}, u32[]{:S(2)}) copy-start(bf16[4096,128]{0,1:T(8,128)(2,1)} %all-gather.11.cloned.1.call-done) | copy-start | bytes 3145732
  240.3 43.5 %copy-start.9 = (bf16[1024,128]{0,1:T(8,128)(2,1)S(1)}, bf16[1024,128]{0,1:T(8,128)(2,1)}, u32[]{:S(2)}) copy-start(bf16[1024,128]{0,1:T(8,128)(2,1)} %slice_select_fusion.1) | copy-start | bytes 786436
  258.8 53.4 %all-gather.13.cloned.1.call-start = ((), (), s32[]{:S(2)}) async-start(), calls=%async_computation.12 | async-start | bytes 1310720 | tf_op jit(solution)/shard_map/all_gather | solution.py:37
  284.8 8.8 %collective-permute-start.1 = (bf16[1024,128]{0,1:T(8,128)(2,1)S(1)}, bf16[1024,128]{0,1:T(8,128)(2,1)S(1)}, u32[]{:S(2)}, u32[]{:S(2)}) collective-permute-start(bf16[1024,128]{0,1:T(8,128)(2,1)S(1)} %add_convert_fusion.5), channel_id=1, source_target_pairs={{0,4},{4,8},{8,12},{1,5},{5,9},{9,13},{2,6},{6,10},{10,14},{3,7},{... | collective-permute-start | bytes 786440 | tf_op jit(solution)/shard_map/ppermute | solution.py:16
  294.3 74.2 %reduce-scatter.12.cloned.1.call-start = ((), (), s32[]{:S(2)}) async-start(), calls=%async_computation.13 | async-start | bytes 1310720 | tf_op jit(solution)/shard_map/reduce_scatter | solution.py:44
  313.7 11.4 %copy-start.2 = (bf16[4096,128]{0,1:T(8,128)(2,1)S(1)}, bf16[4096,128]{0,1:T(8,128)(2,1)}, u32[]{:S(2)}) copy-start(bf16[4096,128]{0,1:T(8,128)(2,1)} %all-gather.13.cloned.1.call-done) | copy-start | bytes 3145732
  325.0 43.5 %copy-start.10 = (bf16[1024,128]{0,1:T(8,128)(2,1)S(1)}, bf16[1024,128]{0,1:T(8,128)(2,1)}, u32[]{:S(2)}) copy-start(bf16[1024,128]{0,1:T(8,128)(2,1)} %slice_select_fusion.2) | copy-start | bytes 786436
  343.6 53.4 %all-gather.15.cloned.1.call-start = ((), (), s32[]{:S(2)}) async-start(), calls=%async_computation.14 | async-start | bytes 1310720 | tf_op jit(solution)/shard_map/all_gather | solution.py:37
  369.5 8.8 %collective-permute-start.2 = (bf16[1024,128]{0,1:T(8,128)(2,1)S(1)}, bf16[1024,128]{0,1:T(8,128)(2,1)S(1)}, u32[]{:S(2)}, u32[]{:S(2)}) collective-permute-start(bf16[1024,128]{0,1:T(8,128)(2,1)S(1)} %add_convert_fusion.4), channel_id=1, source_target_pairs={{0,4},{4,8},{8,12},{1,5},{5,9},{9,13},{2,6},{6,10},{10,14},{3,7},{... | collective-permute-start | bytes 786440 | tf_op jit(solution)/shard_map/ppermute | solution.py:16
  379.1 71.6 %reduce-scatter.14.cloned.1.call-start = ((), (), s32[]{:S(2)}) async-start(), calls=%async_computation.15 | async-start | bytes 1310720 | tf_op jit(solution)/shard_map/reduce_scatter | solution.py:44
  398.5 8.9 %copy-start.3 = (bf16[4096,128]{0,1:T(8,128)(2,1)S(1)}, bf16[4096,128]{0,1:T(8,128)(2,1)}, u32[]{:S(2)}) copy-start(bf16[4096,128]{0,1:T(8,128)(2,1)} %all-gather.15.cloned.1.call-done) | copy-start | bytes 3145732
  407.4 43.3 %copy-start.8 = (bf16[1024,128]{0,1:T(8,128)(2,1)S(1)}, bf16[1024,128]{0,1:T(8,128)(2,1)}, u32[]{:S(2)}) copy-start(bf16[1024,128]{0,1:T(8,128)(2,1)} %slice_select_fusion.3) | copy-start | bytes 786436
  425.8 53.3 %all-gather.17.cloned.1.call-start = ((), (), s32[]{:S(2)}) async-start(), calls=%async_computation.16 | async-start | bytes 1310720 | tf_op jit(solution)/shard_map/all_gather | solution.py:37
  451.7 8.8 %collective-permute-start.3 = (bf16[1024,128]{0,1:T(8,128)(2,1)S(1)}, bf16[1024,128]{0,1:T(8,128)(2,1)S(1)}, u32[]{:S(2)}, u32[]{:S(2)}) collective-permute-start(bf16[1024,128]{0,1:T(8,128)(2,1)S(1)} %add_convert_fusion.3), channel_id=1, source_target_pairs={{0,4},{4,8},{8,12},{1,5},{5,9},{9,13},{2,6},{6,10},{10,14},{3,7},{... | collective-permute-start | bytes 786440 | tf_op jit(solution)/shard_map/ppermute | solution.py:16
  460.5 0.7 copy-start.14
  461.2 71.6 %reduce-scatter.16.cloned.1.call-start = ((), (), s32[]{:S(2)}) async-start(), calls=%async_computation.17 | async-start | bytes 1310720 | tf_op jit(solution)/shard_map/reduce_scatter | solution.py:44
  480.6 8.9 %copy-start.4 = (bf16[4096,128]{0,1:T(8,128)(2,1)S(1)}, bf16[4096,128]{0,1:T(8,128)(2,1)}, u32[]{:S(2)}) copy-start(bf16[4096,128]{0,1:T(8,128)(2,1)} %all-gather.17.cloned.1.call-done) | copy-start | bytes 3145732
  489.5 43.3 %copy-start.15 = (bf16[1024,128]{0,1:T(8,128)(2,1)S(1)}, bf16[1024,128]{0,1:T(8,128)(2,1)}, u32[]{:S(2)}) copy-start(bf16[1024,128]{0,1:T(8,128)(2,1)} %copy-done.14) | copy-start | bytes 786436
  507.9 53.4 %all-gather.19.cloned.1.call-start = ((), (), s32[]{:S(2)}) async-start(), calls=%async_computation.18 | async-start | bytes 1310720 | tf_op jit(solution)/shard_map/all_gather | solution.py:37
  533.8 8.8 %collective-permute-start.4 = (bf16[1024,128]{0,1:T(8,128)(2,1)S(1)}, bf16[1024,128]{0,1:T(8,128)(2,1)S(1)}, u32[]{:S(2)}, u32[]{:S(2)}) collective-permute-start(bf16[1024,128]{0,1:T(8,128)(2,1)S(1)} %add_convert_fusion.2), channel_id=1, source_target_pairs={{0,4},{4,8},{8,12},{1,5},{5,9},{9,13},{2,6},{6,10},{10,14},{3,7},{... | collective-permute-start | bytes 786440 | tf_op jit(solution)/shard_map/ppermute | solution.py:16
  542.6 0.7 copy-start.16
  543.4 71.6 %reduce-scatter.18.cloned.1.call-start = ((), (), s32[]{:S(2)}) async-start(), calls=%async_computation.19 | async-start | bytes 1310720 | tf_op jit(solution)/shard_map/reduce_scatter | solution.py:44
  562.8 8.9 %copy-start.5 = (bf16[4096,128]{0,1:T(8,128)(2,1)S(1)}, bf16[4096,128]{0,1:T(8,128)(2,1)}, u32[]{:S(2)}) copy-start(bf16[4096,128]{0,1:T(8,128)(2,1)} %all-gather.19.cloned.1.call-done) | copy-start | bytes 3145732
  571.7 43.2 %copy-start.17 = (bf16[1024,128]{0,1:T(8,128)(2,1)S(1)}, bf16[1024,128]{0,1:T(8,128)(2,1)}, u32[]{:S(2)}) copy-start(bf16[1024,128]{0,1:T(8,128)(2,1)} %copy-done.16) | copy-start | bytes 786436
  590.0 53.3 %all-gather.21.cloned.1.call-start = ((), (), s32[]{:S(2)}) async-start(), calls=%async_computation.20 | async-start | bytes 1310720 | tf_op jit(solution)/shard_map/all_gather | solution.py:37
  616.0 8.8 %collective-permute-start.5 = (bf16[1024,128]{0,1:T(8,128)(2,1)S(1)}, bf16[1024,128]{0,1:T(8,128)(2,1)S(1)}, u32[]{:S(2)}, u32[]{:S(2)}) collective-permute-start(bf16[1024,128]{0,1:T(8,128)(2,1)S(1)} %add_convert_fusion.1), channel_id=1, source_target_pairs={{0,4},{4,8},{8,12},{1,5},{5,9},{9,13},{2,6},{6,10},{10,14},{3,7},{... | collective-permute-start | bytes 786440 | tf_op jit(solution)/shard_map/ppermute | solution.py:16
  624.8 0.7 copy-start.12
  625.5 71.6 %reduce-scatter.20.cloned.1.call-start = ((), (), s32[]{:S(2)}) async-start(), calls=%async_computation.21 | async-start | bytes 1310720 | tf_op jit(solution)/shard_map/reduce_scatter | solution.py:44
  644.9 8.9 %copy-start.6 = (bf16[4096,128]{0,1:T(8,128)(2,1)S(1)}, bf16[4096,128]{0,1:T(8,128)(2,1)}, u32[]{:S(2)}) copy-start(bf16[4096,128]{0,1:T(8,128)(2,1)} %all-gather.21.cloned.1.call-done) | copy-start | bytes 3145732
  653.8 18.4 %copy-start.19 = (s32[32]{0:T(128)S(1)}, s32[32]{0:T(128)}, u32[]{:S(2)}) copy-start(s32[32]{0:T(128)} %param.11) | copy-start | bytes 388
  653.8 18.4 %copy-start.20 = (s32[4]{0:T(128)S(1)}, s32[4]{0:T(128)}, u32[]{:S(2)}) copy-start(s32[4]{0:T(128)} %param.12) | copy-start | bytes 52
  653.9 43.3 %copy-start.13 = (bf16[1024,128]{0,1:T(8,128)(2,1)S(1)}, bf16[1024,128]{0,1:T(8,128)(2,1)}, u32[]{:S(2)}) copy-start(bf16[1024,128]{0,1:T(8,128)(2,1)} %copy-done.12) | copy-start | bytes 786436
  698.4 11.2 %copy-start.18 = (f32[4096]{0:T(1024)S(1)}, f32[4096]{0:T(1024)}, u32[]{:S(2)}) copy-start(f32[4096]{0:T(1024)} %param.18) | copy-start | bytes 49156
Sparse Core Ops, SparseCore 0:
  69.8 54.8 all-reduce.1
  126.5 15.9 all-gather.8
  174.1 24.7 reduce-scatter.7
  209.6 17.6 all-gather.10
  258.9 24.8 reduce-scatter.9
  294.4 17.6 all-gather.12
  343.7 24.7 reduce-scatter.11
  379.2 17.7 all-gather.14
  425.9 24.7 reduce-scatter.13
  461.3 17.6 all-gather.16
  508.0 24.7 reduce-scatter.15
  543.5 17.7 all-gather.18
  590.2 24.7 reduce-scatter.17
  625.6 17.6 all-gather.20
  672.3 24.7 reduce-scatter.19
where the time goes:
time: 761 us; the launch traced here: 753 us
  waiting for transfers between devices  383 us (50%)
  matrix products  204 us (27%)
  local copies, waits for them, and re-layouts  65.6 us (9%)
  blocking collectives  39.3 us (5%)
  other arithmetic  25.4 us (3%)
  starting transfers between devices  21.7 us (3%)
  between operations  14.2 us (2%)
    reduce_scatter x7, waiting for transfers between devices, layer_split(): lax.psum_scatter(jnp.dot(w_down, hidden, preferred_element_type=jnp.float...  173 us
    dot_general x7, matrix products, layer_split(): jnp.dot(w_down, hidden, preferred_element_type=jnp.float32)  129 us
    all_gather x7, waiting for transfers between devices, layer_split(): wide = lax.all_gather(state, 'mp', axis=0, tiled=True).astype(jnp.float32)  122 us
    dot_general x8, matrix products, contract_rows(): lax.dot_general(weights, acts, (((0,), (0,)), ((), ())), preferred_elemen...  74.6 us
    psum x1, waiting for transfers between devices, per_device(): embedded = lax.psum(partial_value.astype(jnp.bfloat16), 'section')  55 us
    unnamed x45, local copies, waits for them, and re-layouts  46.6 us
    ppermute x6, waiting for transfers between devices, passed_along(): lax.ppermute(value, axis, [(source, source + steps) for source in range(l...  32.2 us
    ppermute x6, starting transfers between devices, passed_along(): lax.ppermute(value, axis, [(source, source + steps) for source in range(l...  20.4 us
  transfers between devices with their start and end apart: 21, of which 21 were waited for; matrix products, arithmetic and copies ran while one was open for 0% of the time, Pallas kernels for 0%

commit v1 on v0

--- a/solution.py
+++ b/solution.py
@@ -1,19 +1,19 @@
+import functools
+
 import jax
 import jax.numpy as jnp
 from jax import lax
+from jax.experimental import pallas as pl
+from jax.experimental.pallas import tpu as pltpu
 from jax.sharding import PartitionSpec as P
 
 GROUP = 8
-
+BATCHES = 2
+CHUNK = 256
 
 norm_eps = 1e-05
 final_eps = 1e-06
-
-
-def passed_along(value, axis, steps):
-    count = lax.axis_size(axis)
-    leading, last = (max(0, -steps), min(count, count - steps))
-    return lax.ppermute(value, axis, [(source, source + steps) for source in range(leading, last)])
+MESH = pl.DeviceIdType.MESH
 
 
 def broadcast(block, axis, source):
@@ -27,27 +27,327 @@
     )
 
 
-def activate(gate_acc, up_acc, squares, width):
-    inverse = lax.rsqrt(squares / width + norm_eps)
-    return (jax.nn.silu(gate_acc * inverse) * (up_acc * inverse)).astype(jnp.bfloat16)
-
-
-def layer_split(state, gain, w_gate, w_up, w_down):
+def pipe_kernel(
+    sections,
+    parts,
+    x0,
+    gain,
+    wg,
+    wu,
+    wd,
+    out,
+    xall,
+    wgb,
+    wub,
+    wdb,
+    accg,
+    accu,
+    hid,
+    xs,
+    sq,
+    sibs,
+    sibr,
+    crs,
+    crr,
+    pown,
+    gsem,
+    usem,
+    dsem,
+    x0sem,
+    zsend,
+    zrecv,
+    agsend,
+    agrecv,
+    fwdsend,
+    sibsend,
+    sibrecv,
+    crsend,
+    crrecv,
+):
+    batches, steps, tokens, chunk = x0.shape
+    chips = parts // 2
+    width = parts * steps * chunk
+    n_fb, _, fb_size = accg.shape
+    sec = lax.axis_index("section")
+    me = lax.axis_index("mp")
+    core = lax.rem(me, 2)
+    chip = lax.div(me, 2)
+    sib = me + 1 - 2 * core
+
+    def peer(d):
+        return lax.rem(chip + d, chips) * 2 + core
+
+    def remote(src, dst, send, recv, target):
+        return pltpu.make_async_remote_copy(
+            src_ref=src,
+            dst_ref=dst,
+            send_sem=send,
+            recv_sem=recv,
+            device_id=target,
+            device_id_type=MESH,
+        )
+
+    def gcopy(i):
+        return pltpu.make_async_copy(wg.at[:, i % steps], wgb.at[i % 2], gsem.at[i % 2])
+
+    def ucopy(i):
+        return pltpu.make_async_copy(wu.at[:, i % steps], wub.at[i % 2], usem.at[i % 2])
+
+    def dcopy(q):
+        return pltpu.make_async_copy(wd.at[:, q], wdb.at[q], dsem.at[q])
+
+    def x0copy(m, q):
+        return pltpu.make_async_copy(x0.at[m, q], xall.at[m, q, me], x0sem.at[m, q])
+
+    def zcopy(m, q):
+        return remote(
+            out.at[m, q], xall.at[m, q, me], zsend.at[m, q], zrecv.at[m, q], {"section": sec + 1}
+        )
+
+    def agcopy(m, q, d):
+        slot = xall.at[m, q, me]
+        target = sib if d == 0 else peer(d)
+        return remote(slot, slot, agsend.at[m, q, d], agrecv.at[m, q, me], {"mp": target})
+
+    def fwdcopy(m, q, d):
+        slot = xall.at[m, q, peer(d)]
+        return remote(slot, slot, fwdsend.at[m, q, d], agrecv.at[m, q, peer(d)], {"mp": sib})
+
+    def agwait(m, q, owner):
+        slot = xall.at[m, q, owner]
+        remote(slot, slot, agsend.at[m, q, 0], agrecv.at[m, q, owner], {"mp": sib}).wait_recv()
+
+    def sibcopy(m, q, c):
+        return remote(
+            sibs.at[m, q, c], sibr.at[m, q, c], sibsend.at[m, q, c], sibrecv.at[m, q, c], {"mp": sib}
+        )
+
+    def crcopy(m, q, d):
+        return remote(
+            crs.at[m, q, d - 1],
+            crr.at[m, q, d - 1],
+            crsend.at[m, q, d - 1],
+            crrecv.at[m, q, d - 1],
+            {"mp": peer(d)},
+        )
+
+    total_steps = batches * steps
+    for i in range(min(2, total_steps)):
+        gcopy(i).start()
+        ucopy(i).start()
+    for q in range(steps):
+        dcopy(q).start()
+
+    @pl.when(sec == 0)
+    def _():
+        for m in range(batches):
+            for q in range(steps):
+                x0copy(m, q).start()
+
+    barrier = pltpu.get_barrier_semaphore()
+    pl.semaphore_signal(barrier, inc=1, device_id={"mp": sib}, device_id_type=MESH)
+    for d in range(1, chips):
+        pl.semaphore_signal(barrier, inc=1, device_id={"mp": peer(d)}, device_id_type=MESH)
+
+    for turn in (1, sections - 1):
+        around = lax.rem(sec + turn, sections)
+        pl.semaphore_signal(barrier, inc=1, device_id={"section": around}, device_id_type=MESH)
+    pl.semaphore_wait(barrier, chips + 2)
+
+    def own_arrive(m, q):
+        @pl.when(sec == 0)
+        def _():
+            x0copy(m, q).wait()
+
+        @pl.when(sec > 0)
+        def _():
+            zcopy(m, q).wait_recv()
+
+        for d in range(1, chips):
+            agcopy(m, q, d).start()
+        agcopy(m, q, 0).start()
+
+    def gate_step(m, q):
+        i = m * steps + q
+        if q + 1 < steps:
+            own_arrive(m, q + 1)
+        for d in range(1, chips):
+            agwait(m, q, peer(d))
+            fwdcopy(m, q, d).start()
+        for c in range(chips):
+            agwait(m, q, 2 * c + 1 - core)
+        squares = jnp.zeros(sq.shape, jnp.float32) if q == 0 else sq[...]
+        lanes = sq.shape[1]
+        for o in range(parts):
+            x = xall[m, q, o].astype(jnp.float32)
+            for lane in range(0, chunk, lanes):
+                piece = x[:, lane : lane + lanes]
+                squares = squares + piece * piece
+            xs[:, o * chunk : (o + 1) * chunk] = (x * gain[o, q]).astype(jnp.bfloat16)
+        sq[...] = squares
+        gcopy(i).wait()
+        ucopy(i).wait()
+
+        def block(fb, carry):
+            cols = pl.ds(pl.multiple_of(fb * fb_size, fb_size), fb_size)
+            for acc, buf in ((accg, wgb), (accu, wub)):
+                w = buf[i % 2, :, :, cols].reshape(parts * chunk, fb_size)
+                term = jnp.dot(xs[...], w, preferred_element_type=jnp.float32)
+                acc[fb] = term if q == 0 else acc[fb] + term
+            return carry
+
+        lax.fori_loop(0, n_fb, block, 0)
+        if i + 2 < total_steps:
+            gcopy(i + 2).start()
+            ucopy(i + 2).start()
+
+    def act_step():
+        mean = jnp.sum(sq[...], axis=1, keepdims=True) / width
+        inverse = lax.rsqrt(mean + norm_eps)
+
+        def block(fb, carry):
+            cols = pl.ds(pl.multiple_of(fb * fb_size, fb_size), fb_size)
+            g = accg[fb] * inverse
+            u = accu[fb] * inverse
+            hid[:, cols] = (g / (1.0 + jnp.exp(-g)) * u).astype(jnp.bfloat16)
+            return carry
+
+        lax.fori_loop(0, n_fb, block, 0)
+
+    def down(q, owner):
+        return lax.dot_general(
+            hid[...], wdb[q, owner], (((1,), (1,)), ((), ())), preferred_element_type=jnp.float32
+        )
+
+    def finish(m, q):
+        sibcopy(m, q, chip).wait_recv()
+        new = pown[q % 2, 0] + sibr[m, q, chip].astype(jnp.float32)
+        for d in range(1, chips):
+            crcopy(m, q, d).wait_recv()
+            new = new + crr[m, q, d - 1].astype(jnp.float32)
+        new = xall[m, q, me].astype(jnp.float32) + new
+        out[m, q] = new.astype(jnp.bfloat16)
+
+        @pl.when(sec < sections - 1)
+        def _():
+            zcopy(m, q).start()
+
+    def down_step(m, q):
+        if m == 0:
+            dcopy(q).wait()
+
+        def to_sibling(c, carry):
+            sibs[m, q, c] = down(q, 2 * c + 1 - core).astype(jnp.bfloat16)
+            sibcopy(m, q, c).start()
+            return carry
+
+        lax.fori_loop(0, chips, to_sibling, 0)
+
+        def to_own(d, carry):
+            pown[q % 2, d] = down(q, peer(d))
+            return carry
+
+        lax.fori_loop(0, chips, to_own, 0)
+        for d in range(1, chips):
+            c = lax.rem(chip + d, chips)
+            sibcopy(m, q, c).wait_recv()
+            both = pown[q % 2, d] + sibr[m, q, c].astype(jnp.float32)
+            crs[m, q, d - 1] = both.astype(jnp.bfloat16)
+            crcopy(m, q, d).start()
+        if q > 0:
+            finish(m, q - 1)
+
+    for m in range(batches):
+        own_arrive(m, 0)
+        for q in range(steps):
+            gate_step(m, q)
+        act_step()
+        for q in range(steps):
+            down_step(m, q)
+        finish(m, steps - 1)
+
+    for m in range(batches):
+        for q in range(steps):
+            for c in range(chips):
+                agcopy(m, q, c).wait_send()
+                sibcopy(m, q, c).wait_send()
+            for d in range(1, chips):
+                fwdcopy(m, q, d).wait_send()
+                crcopy(m, q, d).wait_send()
+
+    @pl.when(sec < sections - 1)
+    def _():
+        for m in range(batches):
+            for q in range(steps):
+                zcopy(m, q).wait_send()
+
+
+def pipeline(embedded, gain, w_gate, w_up, w_down):
+    sections = lax.axis_size("section")
+    parts = lax.axis_size("mp")
+    chips = parts // 2
+    all_tokens, local = embedded.shape
+    hidden = w_gate.shape[1]
     width = gain.shape[0]
-    wide = lax.all_gather(state, "mp", axis=0, tiled=True).astype(jnp.float32)
-    scaled = (wide * gain[:, None]).astype(jnp.bfloat16)
-    gate_acc = contract_rows(w_gate, scaled)
-    up_acc = contract_rows(w_up, scaled)
-    squares = jnp.sum(wide * wide, axis=0, keepdims=True)
-    gate_acc, up_acc, squares = (gate_acc, up_acc, squares)
-    hidden = activate(gate_acc, up_acc, squares, width)
-    mixed = lax.psum_scatter(
-        jnp.dot(w_down, hidden, preferred_element_type=jnp.float32).astype(jnp.bfloat16),
-        "mp",
-        scatter_dimension=0,
-        tiled=True,
-    ).astype(jnp.float32)
-    return (state.astype(jnp.float32) + mixed).astype(jnp.bfloat16)
+    batches = BATCHES
+    tokens = all_tokens // batches
+    chunk = min(CHUNK, local)
+    steps = local // chunk
+    fb_size = next(size for size in (512, 256, 128, hidden) if hidden % size == 0)
+    x0 = embedded.reshape(batches, tokens, steps, chunk).transpose(0, 2, 1, 3)
+    split = (parts, steps, chunk, hidden)
+    bf16, f32 = jnp.bfloat16, jnp.float32
+    vmem = pl.BlockSpec(memory_space=pltpu.VMEM)
+    hbm = pl.BlockSpec(memory_space=pltpu.MemorySpace.HBM)
+    dma = pltpu.SemaphoreType.DMA
+    per_chip = (batches, steps, chips)
+    others = max(1, chips - 1)
+    tile = (tokens, chunk)
+    out = pl.pallas_call(
+        functools.partial(pipe_kernel, sections, parts),
+        out_shape=jax.ShapeDtypeStruct(x0.shape, bf16),
+        in_specs=[vmem, vmem, hbm, hbm, hbm],
+        out_specs=vmem,
+        scratch_shapes=[
+            pltpu.VMEM((batches, steps, parts) + tile, bf16),
+            pltpu.VMEM((2, parts, chunk, hidden), bf16),
+            pltpu.VMEM((2, parts, chunk, hidden), bf16),
+            pltpu.VMEM((steps, parts, chunk, hidden), bf16),
+            pltpu.VMEM((hidden // fb_size, tokens, fb_size), f32),
+            pltpu.VMEM((hidden // fb_size, tokens, fb_size), f32),
+            pltpu.VMEM((tokens, hidden), bf16),
+            pltpu.VMEM((tokens, parts * chunk), bf16),
+            pltpu.VMEM((tokens, min(128, chunk)), f32),
+            pltpu.VMEM(per_chip + tile, bf16),
+            pltpu.VMEM(per_chip + tile, bf16),
+            pltpu.VMEM((batches, steps, others) + tile, bf16),
+            pltpu.VMEM((batches, steps, others) + tile, bf16),
+            pltpu.VMEM((2, chips) + tile, f32),
+            dma((2,)),
+            dma((2,)),
+            dma((steps,)),
+            dma((batches, steps)),
+            dma((batches, steps)),
+            dma((batches, steps)),
+            dma(per_chip),
+            dma((batches, steps, parts)),
+            dma(per_chip),
+            dma(per_chip),
+            dma(per_chip),
+            dma(per_chip),
+            dma(per_chip),
+        ],
+        compiler_params=pltpu.CompilerParams(
+            collective_id=0, has_side_effects=True, vmem_limit_bytes=67043328
+        ),
+    )(
+        x0,
+        gain.reshape(parts, steps, 1, chunk),
+        w_gate.reshape(split),
+        w_up.reshape(split),
+        w_down.reshape(split),
+    )
+    return out.transpose(1, 3, 0, 2).reshape(local, all_tokens)
 
 
 def per_device(
@@ -67,27 +367,13 @@
     vocab_part = embed_table.shape[1]
     flat = token_ids.reshape(-1)
     local_ids = flat - section * vocab_part
-    inside = (local_ids >= 0) & (local_ids < vocab_part)
-    picked = jnp.take(embed_table, jnp.clip(local_ids, 0, vocab_part - 1), axis=1)
-    partial_value = jnp.where(inside[None, :], picked.astype(jnp.float32), 0.0)
-    embedded = lax.psum(partial_value.astype(jnp.bfloat16), "section")
-    gain = norm_gain[0]
-    w_gate = gate_weight[0]
-    w_up = up_weight[0]
-    w_down = down_weight[0]
-    block = embedded.shape[1] // sections
-    state = jnp.zeros((embedded.shape[0], block), jnp.bfloat16)
-    finished = []
-    for tick in range(sections + sections - 1):
-        if tick < sections:
-            fresh = embedded[:, tick * block : (tick + 1) * block]
-            state = jnp.where(section == 0, fresh, state)
-        result = layer_split(state, gain, w_gate, w_up, w_down)
-        if tick >= sections - 1:
-            finished.append(result)
-        if tick < sections + sections - 2:
-            state = passed_along(result, "section", 1)
-    final = jnp.concatenate(finished, axis=1)
+    places = jnp.arange(vocab_part, dtype=jnp.int32)
+    chosen_ids = (local_ids[:, None] == places[None, :]).astype(jnp.bfloat16)
+    picked = lax.dot_general(
+        chosen_ids, embed_table, (((1,), (1,)), ((), ())), preferred_element_type=jnp.float32
+    )
+    embedded = lax.psum(picked.astype(jnp.bfloat16), "section")
+    final = pipeline(embedded, norm_gain[0], gate_weight[0], up_weight[0], down_weight[0])
     responses_here = token_ids.shape[0]
     length = token_ids.shape[1]
     pooled = jnp.mean(

time: 761 us -> 347 us (0.46); the launches traced: 753 us -> 347 us
  waiting for transfers between devices: 383 us -> 53.2 us
  matrix products: 204 us -> 26.8 us
  blocking collectives: 39.3 us -> 144 us
  Pallas kernels: 0 us -> 95.6 us
  local copies, waits for them, and re-layouts: 65.6 us -> 10.7 us
  other arithmetic: 25.4 us -> 3.15 us
  starting transfers between devices: 21.7 us -> 0.01 us
    reduce_scatter x7 -> x0, waiting for transfers between devices: 173 us -> none  [layer_split(): lax.psum_scatter(jnp.dot(w_down, hidden, preferred_element_type=jnp.float...]
    all_gather x7 -> x0, waiting for transfers between devices: 122 us -> none  [layer_split(): wide = lax.all_gather(state, 'mp', axis=0, tiled=True).astype(jnp.float32)]
    dot_general x7 -> x1, matrix products: 129 us -> 21.7 us  [per_device(): lax.dot_general(chosen_ids, embed_table, (((1,), (1,)), ((), ())), prefer...]
    psum x1, blocking collectives: 18.7 us -> 123 us  [broadcast(): return lax.psum(block, axis)]
    pallas_call x0 -> x1, Pallas kernels: none -> 95.6 us  [pipeline(): pl.pallas_call(functools.partial(pipe_kernel, sections, parts), out_shape...]
    dot_general x8 -> x1, matrix products: 74.6 us -> 4.93 us  [contract_rows(): lax.dot_general(weights, acts, (((0,), (0,)), ((), ())), preferred_elemen...]
    unnamed x45 -> x10, local copies, waits for them, and re-layouts: 46.6 us -> 0.41 us
    ppermute x6 -> x0, waiting for transfers between devices: 32.2 us -> none  [passed_along(): lax.ppermute(value, axis, [(source, source + steps) for source in range(l...]
  transfers between devices with their start and end apart: 21 -> 1, of which waited for: 21 -> 1; matrix products, arithmetic and copies ran while one was open for 0% -> 0% of each run, Pallas kernels for 0% -> 0%
where the time goes in v1:
time: 347 us
  blocking collectives  144 us (41%)
  Pallas kernels  95.6 us (28%)
  waiting for transfers between devices  53.2 us (15%)
  matrix products  26.8 us (8%)
  between operations  13.6 us (4%)
  local copies, waits for them, and re-layouts  10.7 us (3%)
    psum x1, blocking collectives, broadcast(): return lax.psum(block, axis)  123 us
    pallas_call x1, Pallas kernels, pipeline(): pl.pallas_call(functools.partial(pipe_kernel, sections, parts), out_shape...  95.6 us
    psum x1, waiting for transfers between devices, per_device(): embedded = lax.psum(picked.astype(jnp.bfloat16), 'section')  53.1 us
    dot_general x1, matrix products, per_device(): lax.dot_general(chosen_ids, embed_table, (((1,), (1,)), ((), ())), prefer...  21.7 us
    psum x1, blocking collectives, per_device(): scores = lax.psum(partial_scores, 'mp')  10.9 us
    all_gather x1, blocking collectives, per_device(): stacked = lax.all_gather(pooled[None], ('dp', 'mp'), axis=0, tiled=True)  9.81 us
  transfers between devices with their start and end apart: 1, of which 1 were waited for; matrix products, arithmetic and copies ran while one was open for 0% of the time, Pallas kernels for 0%

profile of v1, /device:TPU:0, one launch (start us, length us, event | category | flops | bytes accessed | tf_op | source)
XLA Modules:
  0.0 346.8 jit_solution(683862927259287542)
XLA Ops:
  6.5 0.0 all-reduce.2.cloned.1.call-start
  6.5 0.7 broadcast_subtract_fusion
  7.2 0.1 sub.18
  7.3 0.0 copy-start.2
  7.3 0.0 copy-start.3
  7.3 21.7 %fusion.2 = bf16[512,1024]{1,0:T(8,128)(2,1)S(1)} fusion(bf16[1024,16384]{1,0:T(8,128)(2,1)} %param.13, s32[512]{0:T(512)S(1)} %sub.18), kind=kOutput, calls=%fused_computation.6 | convolution fusion | flops 17188782080 | bytes 34605056 | tf_op jit(solution)/shard_map/dot_general | solution.py:372
  29.1 0.8 reshape.83
  29.9 1.2 copy.37
  31.0 0.0 all-reduce.2.cloned.1.call-update
  31.1 0.0 copy-done.2
  31.1 0.1 reshape.86
  31.2 0.0 copy-done.3
  31.2 0.2 fusion.9
  31.4 0.6 gather_fusion
  32.0 0.1 fusion.11
  32.0 0.1 broadcast_or_fusion
  32.1 0.6 reshape.96
  32.7 53.1 %all-reduce.2.cloned.1.call-done.x0 = bf16[2,4,256,256]{3,2,1,0:T(8,128)(2,1)} async-done(((bf16[2,4,256,256]{3,2,1,0:T(8,128)(2,1)}), bf16[2,4,256,256]{3,2,1,0:T(8,128)(2,1)}) %all-reduce.2.cloned.1.call-update) | async-done | bytes 1048592 | tf_op jit(solution)/shard_map/psum | solution.py:375
  85.9 95.6 %shard_map.100 = bf16[2,4,256,256]{3,2,1,0:T(8,128)(2,1)} custom-call(bf16[2,4,256,256]{3,2,1,0:T(8,128)(2,1)} %all-reduce.2.cloned.1.call-done.x0, f32[4,4,1,256]{3,2,1,0:T(1,128)} %bitcast.47, bf16[4,4,256,2560]{3,2,1,0:T(8,128)(2,1)} %bitcast.40, bf16[4,4,256,2560]{3,2,1,0:T(8,128)(2,1)} %bitcast.41, bf16[4,4,256,2560]{3,2,1,0:T(8,128)(2,1)} %bitcast.42), custom_call_target="tpu_custom_call" | custom-call | tf_op jit(solution)/shard_map/pallas_call | solution.py:306
  181.5 0.0 copy-start.1
  181.5 1.4 convert_bitcast_fusion
  182.9 2.7 copy.30
  185.6 2.3 reshape.87
  187.9 0.3 reduce_sum.29
  188.3 9.8 %all-gather = f32[8192,16]{0,1:T(8,128)S(1)} all-gather(f32[1024,16]{0,1:T(8,128)S(1)} %broadcast_multiply_fusion), channel_id=2, replica_groups=mesh['dp'=2,'section'=4,'mp'=4] {'dp','mp'}, dimensions={0}, use_global_device_ids=true | all-gather | bytes 589824 | tf_op jit(solution)/shard_map/all_gather | solution.py:384
  198.1 0.3 reshape.84
  198.4 0.2 multiply_reduce_fusion
  198.7 0.3 copy.34
  199.0 0.1 copy.35
  199.1 0.1 rsqrt.12
  199.2 0.0 copy-done.1
  199.2 0.0 copy-start
  199.2 0.1 multiply_convert_fusion
  199.3 4.9 %fusion.16 = f32[32,1024]{1,0:T(8,128)S(1)} fusion(bf16[4096,32]{0,1:T(8,128)(2,1)S(1)} %multiply_convert_fusion, bf16[4096,1024]{1,0:T(8,128)(2,1)} %param.19), kind=kOutput, calls=%fused_computation.35 | convolution fusion | flops 268435456 | bytes 8781824 | tf_op jit(solution)/shard_map/dot_general | solution.py:25
  204.2 0.2 fusion.3
  204.4 10.9 %psum.22 = f32[32,32]{1,0:T(8,128)S(1)} all-reduce(f32[32,32]{1,0:T(8,128)S(1)} %fusion.3), channel_id=1, replica_groups=mesh['dp'=2,'section'=4,'mp'=4] {'mp'}, use_global_device_ids=true, to_apply=%region_3.0 | all-reduce | flops 1024 | bytes 8192 | tf_op jit(solution)/shard_map/psum | solution.py:403
  215.3 123.1 %psum.23 = f32[32,32]{1,0:T(8,128)S(1)} all-reduce(f32[32,32]{1,0:T(8,128)S(1)} %broadcast_select_fusion), channel_id=1, replica_groups=mesh['dp'=2,'section'=4,'mp'=4] {'section'}, use_global_device_ids=true, to_apply=%region_4.5 | all-reduce | flops 1024 | bytes 8192 | tf_op jit(solution)/shard_map/psum | solution.py:21
  338.4 0.1 copy.33
  338.5 0.0 copy-done
  338.6 0.7 gather_fusion.1
  339.3 0.7 reshape.99
  (9 shorter events, 0.1 us)
Async XLA Ops:
  6.5 79.3 %all-reduce.2.cloned.1.call-start = ((), (), s32[]{:S(2)}) async-start(), calls=%async_computation | async-start | bytes 2097152 | tf_op jit(solution)/shard_map/psum | solution.py:375
  7.3 23.8 %copy-start.2 = (s32[32]{0:T(128)S(1)}, s32[32]{0:T(128)}, u32[]{:S(2)}) copy-start(s32[32]{0:T(128)} %param.11) | copy-start | bytes 388
  7.3 23.9 %copy-start.3 = (s32[4]{0:T(128)S(1)}, s32[4]{0:T(128)}, u32[]{:S(2)}) copy-start(s32[4]{0:T(128)} %param.12) | copy-start | bytes 52
  181.5 17.7 %copy-start.1 = (f32[4096]{0:T(1024)S(1)}, f32[4096]{0:T(1024)}, u32[]{:S(2)}) copy-start(f32[4096]{0:T(1024)} %param.18) | copy-start | bytes 49156
  199.2 139.4 %copy-start = (s32[32]{0:T(128)S(1)}, s32[32]{0:T(128)}, u32[]{:S(2)}) copy-start(s32[32]{0:T(128)} %reshape.96) | copy-start | bytes 388
Sparse Core Ops, SparseCore 0:
  31.2 54.6 all-reduce.1

commit v2 on v1

--- a/solution.py
+++ b/solution.py
@@ -14,11 +14,6 @@
 norm_eps = 1e-05
 final_eps = 1e-06
 MESH = pl.DeviceIdType.MESH
-
-
-def broadcast(block, axis, source):
-    block = jnp.where(lax.axis_index(axis) == source, block, jnp.zeros_like(block))
-    return lax.psum(block, axis)
 
 
 def contract_rows(weights, acts):
@@ -35,6 +30,7 @@
     wg,
     wu,
     wd,
+    pooled,
     out,
     xall,
     wgb,
@@ -53,7 +49,9 @@
     gsem,
     usem,
     dsem,
-    x0sem,
+    ering,
+    esend,
+    erecv,
     zsend,
     zrecv,
     agsend,
@@ -96,8 +94,9 @@
     def dcopy(q):
         return pltpu.make_async_copy(wd.at[:, q], wdb.at[q], dsem.at[q])
 
-    def x0copy(m, q):
-        return pltpu.make_async_copy(x0.at[m, q], xall.at[m, q, me], x0sem.at[m, q])
+    def ecopy(m, q, src):
+        target = {"section": sec - 1}
+        return remote(src, ering.at[m, q], esend.at[m, q], erecv.at[m, q], target)
 
     def zcopy(m, q):
         return remote(
@@ -138,12 +137,6 @@
     for q in range(steps):
         dcopy(q).start()
 
-    @pl.when(sec == 0)
-    def _():
-        for m in range(batches):
-            for q in range(steps):
-                x0copy(m, q).start()
-
     barrier = pltpu.get_barrier_semaphore()
     pl.semaphore_signal(barrier, inc=1, device_id={"mp": sib}, device_id_type=MESH)
     for d in range(1, chips):
@@ -157,7 +150,11 @@
     def own_arrive(m, q):
         @pl.when(sec == 0)
         def _():
-            x0copy(m, q).wait()
+            if sections > 1:
+                ecopy(m, q, x0.at[m, q]).wait_recv()
+                xall[m, q, me] = ering[m, q] + x0[m, q]
+            else:
+                xall[m, q, me] = x0[m, q]
 
         @pl.when(sec > 0)
         def _():
@@ -226,7 +223,11 @@
             crcopy(m, q, d).wait_recv()
             new = new + crr[m, q, d - 1].astype(jnp.float32)
         new = xall[m, q, me].astype(jnp.float32) + new
-        out[m, q] = new.astype(jnp.bfloat16)
+        rounded = new.astype(jnp.bfloat16)
+        out[m, q] = rounded
+        here = pooled.shape[2]
+        grouped = rounded.astype(jnp.float32).reshape(here, tokens // here, chunk)
+        pooled[m, q] = jnp.sum(grouped, axis=1) / (tokens // here)
 
         @pl.when(sec < sections - 1)
         def _():
@@ -257,6 +258,21 @@
         if q > 0:
             finish(m, q - 1)
 
+    pairs = [(m, q) for m in range(batches) for q in range(steps)]
+
+    @pl.when(sec == sections - 1)
+    def _():
+        for m, q in pairs:
+            if sections > 1:
+                ecopy(m, q, x0.at[m, q]).start()
+
+    @pl.when((sec > 0) & (sec < sections - 1))
+    def _():
+        for m, q in pairs:
+            ecopy(m, q, x0.at[m, q]).wait_recv()
+            ering[m, q] = ering[m, q] + x0[m, q]
+            ecopy(m, q, ering.at[m, q]).start()
+
     for m in range(batches):
         own_arrive(m, 0)
         for q in range(steps):
@@ -277,12 +293,16 @@
 
     @pl.when(sec < sections - 1)
     def _():
-        for m in range(batches):
-            for q in range(steps):
-                zcopy(m, q).wait_send()
-
-
-def pipeline(embedded, gain, w_gate, w_up, w_down):
+        for m, q in pairs:
+            zcopy(m, q).wait_send()
+
+    @pl.when(sec > 0)
+    def _():
+        for m, q in pairs:
+            ecopy(m, q, x0.at[m, q]).wait_send()
+
+
+def pipeline(embedded, gain, w_gate, w_up, w_down, responses):
     sections = lax.axis_size("section")
     parts = lax.axis_size("mp")
     chips = parts // 2
@@ -303,12 +323,13 @@
     per_chip = (batches, steps, chips)
     others = max(1, chips - 1)
     tile = (tokens, chunk)
-    out = pl.pallas_call(
+    pooled = pl.pallas_call(
         functools.partial(pipe_kernel, sections, parts),
-        out_shape=jax.ShapeDtypeStruct(x0.shape, bf16),
+        out_shape=jax.ShapeDtypeStruct((batches, steps, responses // batches, chunk), f32),
         in_specs=[vmem, vmem, hbm, hbm, hbm],
         out_specs=vmem,
         scratch_shapes=[
+            pltpu.VMEM(x0.shape, bf16),
             pltpu.VMEM((batches, steps, parts) + tile, bf16),
             pltpu.VMEM((2, parts, chunk, hidden), bf16),
             pltpu.VMEM((2, parts, chunk, hidden), bf16),
@@ -326,6 +347,8 @@
             dma((2,)),
             dma((2,)),
             dma((steps,)),
+            pltpu.VMEM(x0.shape, bf16),
+            dma((batches, steps)),
             dma((batches, steps)),
             dma((batches, steps)),
             dma((batches, steps)),
@@ -347,7 +370,7 @@
         w_up.reshape(split),
         w_down.reshape(split),
     )
-    return out.transpose(1, 3, 0, 2).reshape(local, all_tokens)
+    return pooled.transpose(1, 3, 0, 2).reshape(local, responses)
 
 
 def per_device(
@@ -372,13 +395,15 @@
     picked = lax.dot_general(
         chosen_ids, embed_table, (((1,), (1,)), ((), ())), preferred_element_type=jnp.float32
     )
-    embedded = lax.psum(picked.astype(jnp.bfloat16), "section")
-    final = pipeline(embedded, norm_gain[0], gate_weight[0], up_weight[0], down_weight[0])
+    pooled = pipeline(
+        picked.astype(jnp.bfloat16),
+        norm_gain[0],
+        gate_weight[0],
+        up_weight[0],
+        down_weight[0],
+        token_ids.shape[0],
+    )
     responses_here = token_ids.shape[0]
-    length = token_ids.shape[1]
-    pooled = jnp.mean(
-        final.astype(jnp.float32).reshape(final.shape[0], responses_here, length), axis=2
-    )
     groups_count = lax.axis_size("dp")
     parts = lax.axis_size("mp")
     stacked = lax.all_gather(pooled[None], ("dp", "mp"), axis=0, tiled=True)
@@ -400,8 +425,10 @@
         precision=lax.Precision.HIGHEST,
         preferred_element_type=jnp.float32,
     )
-    scores = lax.psum(partial_scores, "mp")
-    scores = broadcast(scores, "section", sections - 1)
+    scores = lax.psum(
+        jnp.where(section == sections - 1, partial_scores, jnp.zeros_like(partial_scores)),
+        ("section", "mp"),
+    )
     preference = jax.nn.sigmoid(scores - scores.T)
     prompt_count = owners.shape[0]
     local_prompts = prompt_count // lax.axis_size("dp")

time: 347 us -> 324 us (0.934)
  waiting for transfers between devices: 53.2 us -> 0 us
  blocking collectives: 144 us -> 176 us
  Pallas kernels: 95.6 us -> 112 us
  between operations: 13.6 us -> 0.07 us
  local copies, waits for them, and re-layouts: 10.7 us -> 5.57 us
    psum x1 -> x0, waiting for transfers between devices: 53.1 us -> none  [per_device(): embedded = lax.psum(picked.astype(jnp.bfloat16), 'section')]
    psum x2 -> x1, blocking collectives: 134 us -> 166 us  [per_device(): lax.psum(jnp.where(section == sections - 1, partial_scores, jnp.zeros_lik...]
    pallas_call x1, Pallas kernels: 95.6 us -> 112 us  [pipeline(): pl.pallas_call(functools.partial(pipe_kernel, sections, parts), out_shape...]
    convert_element_type x2 -> x0, local copies, waits for them, and re-layouts: 5.03 us -> none  [per_device(): final.astype(jnp.float32).reshape(final.shape[0], responses_here, length)]
  transfers between devices with their start and end apart: 1 -> 0, of which waited for: 1 -> 0; matrix products, arithmetic and copies ran while one was open for 0% -> 0% of each run, Pallas kernels for 0% -> 0%
where the time goes in v2:
time: 324 us; the launch traced here: 323 us
  blocking collectives  176 us (54%)
  Pallas kernels  112 us (35%)
  matrix products  26.8 us (8%)
  local copies, waits for them, and re-layouts  5.57 us (2%)
    psum x1, blocking collectives, per_device(): lax.psum(jnp.where(section == sections - 1, partial_scores, jnp.zeros_lik...  166 us
    pallas_call x1, Pallas kernels, pipeline(): pl.pallas_call(functools.partial(pipe_kernel, sections, parts), out_shape...  112 us
    dot_general x1, matrix products, per_device(): lax.dot_general(chosen_ids, embed_table, (((1,), (1,)), ((), ())), prefer...  21.7 us
    all_gather x1, blocking collectives, per_device(): stacked = lax.all_gather(pooled[None], ('dp', 'mp'), axis=0, tiled=True)  9.86 us

profile of v2, /device:TPU:0, one launch (start us, length us, event | category | flops | bytes accessed | tf_op | source)
XLA Modules:
  0.0 323.5 jit_solution(15293382206362160394)
XLA Ops:
  0.0 0.7 broadcast_subtract_fusion
  0.7 0.1 sub.18
  0.8 21.7 %fusion.2 = bf16[512,1024]{1,0:T(8,128)(2,1)S(1)} fusion(bf16[1024,16384]{1,0:T(8,128)(2,1)} %param.13, s32[512]{0:T(512)S(1)} %sub.18), kind=kOutput, calls=%fused_computation.5 | convolution fusion | flops 17188782080 | bytes 34605056 | tf_op jit(solution)/shard_map/dot_general | solution.py:395
  22.5 0.8 reshape.69
  23.3 1.1 copy.24
  24.4 111.8 %shard_map.100 = f32[2,4,8,256]{3,2,1,0:T(8,128)} custom-call(bf16[2,4,256,256]{3,2,1,0:T(8,128)(2,1)} %bitcast.45, f32[4,4,1,256]{3,2,1,0:T(1,128)} %bitcast.49, bf16[4,4,256,2560]{3,2,1,0:T(8,128)(2,1)} %bitcast.40, bf16[4,4,256,2560]{3,2,1,0:T(8,128)(2,1)} %bitcast.41, bf16[4,4,256,2560]{3,2,1,0:T(8,128)(2,1)} %bitcast.42), custom_call_target="tpu_custom_call" | custom-call | tf_op jit(solution)/shard_map/pallas_call | solution.py:326
  136.3 9.9 %all_gather.3 = f32[8,1024,16]{1,2,0:T(8,128)S(1)} all-gather(f32[1,1024,16]{1,2,0:T(8,128)} %bitcast.48), channel_id=1, replica_groups=mesh['dp'=2,'section'=4,'mp'=4] {'dp','mp'}, dimensions={0}, use_global_device_ids=true | all-gather | bytes 589824 | tf_op jit(solution)/shard_map/all_gather | solution.py:409
  146.1 0.3 copy.19
  146.5 0.3 copy.21
  146.8 0.5 fusion.3
  147.2 0.1 rsqrt.12
  147.3 0.8 multiply_convert_fusion
  148.2 4.9 %fusion.16 = f32[32,1024]{1,0:T(8,128)S(1)} fusion(bf16[4096,32]{0,1:T(8,128)(2,1)S(1)} %multiply_convert_fusion, bf16[4096,1024]{1,0:T(8,128)(2,1)} %param.19), kind=kOutput, calls=%fused_computation.33 | convolution fusion | flops 268435456 | bytes 8781824 | tf_op jit(solution)/shard_map/dot_general | solution.py:20
  153.1 0.2 convolution_select_fusion
  153.3 166.3 %psum.7 = f32[32,32]{1,0:T(8,128)S(1)} all-reduce(f32[32,32]{1,0:T(8,128)S(1)} %convolution_select_fusion), channel_id=1, replica_groups=mesh['dp'=2,'section'=4,'mp'=4] {'section','mp'}, use_global_device_ids=true, to_apply=%region_1.2 | all-reduce | flops 1024 | bytes 8192 | tf_op jit(solution)/shard_map/psum | solution.py:428
  319.6 0.1 copy.20
  319.7 0.7 reshape.72
  320.4 0.8 fusion.9
  321.3 0.6 gather_fusion
  321.9 0.1 fusion.11
  322.0 0.1 broadcast_or_fusion
  322.0 0.1 reshape.81
  322.1 0.7 gather_fusion.1
  322.8 0.7 reshape.84
  (6 shorter events, 0.1 us)

commit v3 on v2

--- a/solution.py
+++ b/solution.py
@@ -85,11 +85,34 @@
             device_id_type=MESH,
         )
 
+    def order(m):
+        return list(range(steps)) if m % 2 == 0 else list(range(steps))[::-1]
+
+    visits = [q for m in range(batches) for q in order(m)]
+    held = [None, None]
+    slots, fresh = [], []
+    for i, q in enumerate(visits):
+        fresh.append(q not in held)
+        if q not in held:
+            free = [n for n in range(2) if held[n] not in visits[i - 1 : i] or held[n] is None]
+            held[free[0]] = q
+        slots.append(held.index(q))
+
     def gcopy(i):
-        return pltpu.make_async_copy(wg.at[:, i % steps], wgb.at[i % 2], gsem.at[i % 2])
+        slot = slots[i]
+        return pltpu.make_async_copy(wg.at[:, visits[i]], wgb.at[slot], gsem.at[slot])
 
     def ucopy(i):
-        return pltpu.make_async_copy(wu.at[:, i % steps], wub.at[i % 2], usem.at[i % 2])
+        slot = slots[i]
+        return pltpu.make_async_copy(wu.at[:, visits[i]], wub.at[slot], usem.at[slot])
+
+    def load_into(slot, after):
+        for i in range(after, len(visits)):
+            if slots[i] == slot:
+                if fresh[i]:
+                    gcopy(i).start()
+                    ucopy(i).start()
+                return
 
     def dcopy(q):
         return pltpu.make_async_copy(wd.at[:, q], wdb.at[q], dsem.at[q])
@@ -130,12 +153,8 @@
             {"mp": peer(d)},
         )
 
-    total_steps = batches * steps
-    for i in range(min(2, total_steps)):
-        gcopy(i).start()
-        ucopy(i).start()
-    for q in range(steps):
-        dcopy(q).start()
+    for slot in range(2):
+        load_into(slot, 0)
 
     barrier = pltpu.get_barrier_semaphore()
     pl.semaphore_signal(barrier, inc=1, device_id={"mp": sib}, device_id_type=MESH)
@@ -164,16 +183,17 @@
             agcopy(m, q, d).start()
         agcopy(m, q, 0).start()
 
-    def gate_step(m, q):
-        i = m * steps + q
-        if q + 1 < steps:
-            own_arrive(m, q + 1)
+    def gate_step(m, turn):
+        i = m * steps + turn
+        q, slot = visits[i], slots[i]
+        if turn + 1 < steps:
+            own_arrive(m, visits[i + 1])
         for d in range(1, chips):
             agwait(m, q, peer(d))
             fwdcopy(m, q, d).start()
         for c in range(chips):
             agwait(m, q, 2 * c + 1 - core)
-        squares = jnp.zeros(sq.shape, jnp.float32) if q == 0 else sq[...]
+        squares = jnp.zeros(sq.shape, jnp.float32) if turn == 0 else sq[...]
         lanes = sq.shape[1]
         for o in range(parts):
             x = xall[m, q, o].astype(jnp.float32)
@@ -182,21 +202,23 @@
                 squares = squares + piece * piece
             xs[:, o * chunk : (o + 1) * chunk] = (x * gain[o, q]).astype(jnp.bfloat16)
         sq[...] = squares
-        gcopy(i).wait()
-        ucopy(i).wait()
+        if fresh[i]:
+            gcopy(i).wait()
+            ucopy(i).wait()
 
         def block(fb, carry):
             cols = pl.ds(pl.multiple_of(fb * fb_size, fb_size), fb_size)
             for acc, buf in ((accg, wgb), (accu, wub)):
-                w = buf[i % 2, :, :, cols].reshape(parts * chunk, fb_size)
+                w = buf[slot, :, :, cols].reshape(parts * chunk, fb_size)
                 term = jnp.dot(xs[...], w, preferred_element_type=jnp.float32)
-                acc[fb] = term if q == 0 else acc[fb] + term
+                acc[fb] = term if turn == 0 else acc[fb] + term
             return carry
 
         lax.fori_loop(0, n_fb, block, 0)
-        if i + 2 < total_steps:
-            gcopy(i + 2).start()
-            ucopy(i + 2).start()
+        load_into(slot, i + 1)
+        if m == 0 and turn == min(1, steps - 1):
+            for other in range(steps):
+                dcopy(other).start()
 
     def act_step():
         mean = jnp.sum(sq[...], axis=1, keepdims=True) / width
@@ -233,7 +255,8 @@
         def _():
             zcopy(m, q).start()
 
-    def down_step(m, q):
+    def down_step(m, turn):
+        q = order(m)[turn]
         if m == 0:
             dcopy(q).wait()
 
@@ -255,10 +278,10 @@
             both = pown[q % 2, d] + sibr[m, q, c].astype(jnp.float32)
             crs[m, q, d - 1] = both.astype(jnp.bfloat16)
             crcopy(m, q, d).start()
-        if q > 0:
-            finish(m, q - 1)
-
-    pairs = [(m, q) for m in range(batches) for q in range(steps)]
+        if turn > 0:
+            finish(m, order(m)[turn - 1])
+
+    pairs = [(m, q) for m in range(batches) for q in order(m)]
 
     @pl.when(sec == sections - 1)
     def _():
@@ -274,13 +297,13 @@
             ecopy(m, q, ering.at[m, q]).start()
 
     for m in range(batches):
-        own_arrive(m, 0)
-        for q in range(steps):
-            gate_step(m, q)
+        own_arrive(m, order(m)[0])
+        for turn in range(steps):
+            gate_step(m, turn)
         act_step()
-        for q in range(steps):
-            down_step(m, q)
-        finish(m, steps - 1)
+        for turn in range(steps):
+            down_step(m, turn)
+        finish(m, order(m)[-1])
 
     for m in range(batches):
         for q in range(steps):
@@ -425,10 +448,8 @@
         precision=lax.Precision.HIGHEST,
         preferred_element_type=jnp.float32,
     )
-    scores = lax.psum(
-        jnp.where(section == sections - 1, partial_scores, jnp.zeros_like(partial_scores)),
-        ("section", "mp"),
-    )
+    shares = lax.all_gather(partial_scores[None], ("section", "mp"), axis=0, tiled=True)
+    scores = jnp.sum(shares[(sections - 1) * parts :], axis=0)
     preference = jax.nn.sigmoid(scores - scores.T)
     prompt_count = owners.shape[0]
     local_prompts = prompt_count // lax.axis_size("dp")

time: 324 us -> 290 us (0.90)
  blocking collectives: 176 us -> 140 us
    psum x1 -> x0, blocking collectives: 166 us -> none  [per_device(): lax.psum(jnp.where(section == sections - 1, partial_scores, jnp.zeros_lik...]
    all_gather x0 -> x1, blocking collectives: none -> 130 us  [per_device(): lax.all_gather(partial_scores[None], ('section', 'mp'), axis=0, tiled=True)]
where the time goes in v3:
time: 290 us; the launch traced here: 289 us
  blocking collectives  140 us (48%)
  Pallas kernels  113 us (39%)
  matrix products  26.8 us (9%)
  local copies, waits for them, and re-layouts  6.21 us (2%)
  other arithmetic  3.04 us (1%)
    all_gather x1, blocking collectives, per_device(): lax.all_gather(partial_scores[None], ('section', 'mp'), axis=0, tiled=True)  130 us
    pallas_call x1, Pallas kernels, pipeline(): pl.pallas_call(functools.partial(pipe_kernel, sections, parts), out_shape...  113 us
    dot_general x1, matrix products, per_device(): lax.dot_general(chosen_ids, embed_table, (((1,), (1,)), ((), ())), prefer...  21.7 us
    all_gather x1, blocking collectives, per_device(): stacked = lax.all_gather(pooled[None], ('dp', 'mp'), axis=0, tiled=True)  9.86 us

profile of v3, /device:TPU:0, one launch (start us, length us, event | category | flops | bytes accessed | tf_op | source)
XLA Modules:
  0.0 289.5 jit_solution(4042898385674452148)
XLA Ops:
  0.0 0.8 fusion.10
  0.8 0.7 reshape.72
  1.6 0.6 gather_fusion
  2.2 0.1 fusion.12
  2.2 0.1 broadcast_or_fusion
  2.3 0.6 reshape.81
  2.9 0.7 broadcast_subtract_fusion
  3.6 0.1 sub.18
  3.7 21.7 %fusion.2 = bf16[512,1024]{1,0:T(8,128)(2,1)S(1)} fusion(bf16[1024,16384]{1,0:T(8,128)(2,1)} %param.13, s32[512]{0:T(512)S(1)} %sub.18), kind=kOutput, calls=%fused_computation.5 | convolution fusion | flops 17188782080 | bytes 34605056 | tf_op jit(solution)/shard_map/dot_general | solution.py:418
  25.4 0.8 reshape.69
  26.2 1.1 copy.24
  27.3 113.4 %shard_map.100 = f32[2,4,8,256]{3,2,1,0:T(8,128)} custom-call(bf16[2,4,256,256]{3,2,1,0:T(8,128)(2,1)} %bitcast.46, f32[4,4,1,256]{3,2,1,0:T(1,128)} %bitcast.51, bf16[4,4,256,2560]{3,2,1,0:T(8,128)(2,1)} %bitcast.41, bf16[4,4,256,2560]{3,2,1,0:T(8,128)(2,1)} %bitcast.42, bf16[4,4,256,2560]{3,2,1,0:T(8,128)(2,1)} %bitcast.43), custom_call_target="tpu_custom_call" | custom-call | tf_op jit(solution)/shard_map/pallas_call | solution.py:349
  140.8 9.9 %all_gather.6 = f32[8,1024,16]{1,2,0:T(8,128)S(1)} all-gather(f32[1,1024,16]{1,2,0:T(8,128)} %bitcast.50), channel_id=1, replica_groups=mesh['dp'=2,'section'=4,'mp'=4] {'dp','mp'}, dimensions={0}, use_global_device_ids=true | all-gather | bytes 589824 | tf_op jit(solution)/shard_map/all_gather | solution.py:432
  150.6 0.5 fusion.3
  151.1 0.3 copy.19
  151.4 0.3 copy.21
  151.8 0.1 rsqrt.12
  151.9 0.8 multiply_convert_fusion
  152.7 4.9 %fusion.17 = f32[32,1024]{1,0:T(8,128)S(1)} fusion(bf16[4096,32]{0,1:T(8,128)(2,1)S(1)} %multiply_convert_fusion, bf16[4096,1024]{1,0:T(8,128)(2,1)} %param.19), kind=kOutput, calls=%fused_computation.33 | convolution fusion | flops 268435456 | bytes 8781824 | tf_op jit(solution)/shard_map/dot_general | solution.py:20
  157.6 0.2 fusion.4
  157.8 130.0 %all-gather = f32[512,32]{1,0:T(8,128)S(1)} all-gather(f32[32,32]{1,0:T(8,128)S(1)} %fusion.4), channel_id=2, replica_groups=mesh['dp'=2,'section'=4,'mp'=4] {'section','mp'}, dimensions={0}, use_global_device_ids=true | all-gather | bytes 69632 | tf_op jit(solution)/shard_map/all_gather | solution.py:451
  287.9 0.1 copy.20
  287.9 0.8 gather_fusion.1
  288.8 0.7 reshape.84
  (8 shorter events, 0.1 us)
